TPU v7x, 128 devices: a whole 4x4x4 slice. The times are simulated.
128 devices in a mesh: grp: 8 (over z, core), sub: 16 (over x, y).
Axes of the slice: x: 4, y: 4, z: 4, core: 2. Of those that a mesh axis runs over, the one named last changes fastest.
Arguments:
- rhs: float32 [96, 131072], P(None, ('grp', 'sub')), may hold values from -13 to 13
- blocks: bfloat16 [16384, 6656], P(('grp', 'sub')), may hold values from -0.05 to 0.45, as said below
- owners: int32 [16384, 1], P(('grp', 'sub')), may hold values from 0 to 7; in each aligned block of 128 rows (0 to 127, 128 to 255, ...) at most 48 rows name the same one
- conn: int32 [16384, 27], P(('grp', 'sub')), may hold values from 0 to 16383, as said below
Outputs:
- solution: float32 [96, 131072], P(None, ('grp', 'sub'))
- residual: float32 [96, 131072], P(None, ('grp', 'sub'))
Inputs may be any that keep to these rules, and one draw needn't show every extreme that they name: `blocks`: entries at positions 6561 and beyond are zero. `owners`: in each device's 128 rows at most 48 name the same column. `conn`: A column's nodes form layers of 128 nodes, node n in layer n // 128. An element in the rows of the device at position s along sub touches three consecutive layers, all within nodes s * 1024 to (s + 1) * 1024 + 2 * 128 - 1 of its column (within the column).
All inputs are finite; a program needn't handle non-finite values.
Results may differ from a plain program's by a relative error of at most 0.0075.
Values may be sent and summed in bfloat16 or wider, within the bound.
A program may use at most 192 MiB of HBM per device.

v0:
```python
import jax
import jax.numpy as jnp
from jax import lax
from jax.sharding import PartitionSpec as P

STEPS = 2
epsilon = 1e-06


def passed_along(block, axis, distance):
    devices = range(lax.axis_size(axis))
    route = [(i - distance, i) for i in devices if i - distance in devices]
    return lax.ppermute(block, axis, route)


def place_blocks(blocks, owners, conn, groups, capacity):
    owner_group = owners[:, 0]
    onehot = (owner_group[:, None] == jnp.arange(groups, dtype=jnp.int32)[None, :]).astype(
        jnp.int32
    )
    before = jnp.cumsum(onehot, axis=0) - onehot
    position = jnp.sum(before * onehot, axis=1)
    target = owner_group * capacity + position
    send_blocks = (
        jnp.zeros((groups * capacity, blocks.shape[1]), blocks.dtype).at[target].set(blocks)
    )
    send_links = jnp.zeros((groups * capacity, conn.shape[1]), jnp.int32).at[target].set(conn)
    return (send_blocks.reshape(groups, capacity, -1), send_links.reshape(groups, capacity, -1))


def window_product(matrix_groups, link_groups, field):
    rows = field.shape[0]
    window = field.shape[1]
    places = jnp.arange(window, dtype=jnp.int32)

    def one_group(acc, pair):
        matrix, links = pair
        slot_count = matrix.shape[0]
        selector = (links[:, None] == places[None, :]).astype(jnp.bfloat16)
        picked = jnp.einsum(
            "rw,lw->rl", field, selector, preferred_element_type=jnp.float32
        ).astype(jnp.bfloat16)
        picked = picked.reshape(3, rows // 3, slot_count, 27)
        result = jnp.einsum("spcqd,cosp->dosq", matrix, picked, preferred_element_type=jnp.float32)
        result = result.reshape(rows, slot_count * 27)
        high_part = result.astype(jnp.bfloat16)
        low_part = (result - high_part.astype(jnp.float32)).astype(jnp.bfloat16)
        acc = acc + jnp.dot(high_part, selector, preferred_element_type=jnp.float32)
        acc = acc + jnp.dot(low_part, selector, preferred_element_type=jnp.float32)
        return (acc, None)

    start = jnp.zeros((rows, window), jnp.float32)
    acc, unused = lax.scan(one_group, start, (matrix_groups, link_groups))
    return acc


def column_sums(first, second):
    return jnp.sum((first * second).reshape(3, -1, first.shape[1]), axis=(0, 2))


def update(solution, residual, image, along, energy):
    alpha = along / (energy + epsilon)
    scale_rows = jnp.tile(alpha, 3)[:, None]
    return (solution + scale_rows * residual, residual - scale_rows * image)


def shards(rhs, blocks, owners, conn):
    groups = lax.axis_size("grp")
    held = blocks.shape[0]
    capacity = max(2, 3 * held // 8)
    send_blocks, send_links = place_blocks(blocks, owners, conn, groups, capacity)
    got_blocks, got_links = (
        lax.all_to_all(send_blocks, "grp", split_axis=0, concat_axis=0, tiled=True),
        lax.all_to_all(send_links, "grp", split_axis=0, concat_axis=0, tiled=True),
    )
    matrix_groups = got_blocks[:, :, :6561].reshape(groups, capacity, 27, 3, 27, 3)
    residual = rhs
    solution = jnp.zeros(rhs.shape, jnp.float32)
    own_count = rhs.shape[1]
    band_width = 2 * held
    local_links = jnp.clip(
        got_links - lax.axis_index("sub") * own_count, 0, own_count + band_width - 1
    ).astype(jnp.int32)
    link_groups = local_links.reshape(groups, capacity * 27)
    for step in range(STEPS):
        rounded = residual.astype(jnp.bfloat16)
        upper = passed_along(rounded[:, :band_width], "sub", -1)
        field = jnp.concatenate([rounded, upper], axis=1)
        partial_sum = window_product(matrix_groups, link_groups, field)
        incoming = passed_along(partial_sum[:, own_count:], "sub", 1)
        image = partial_sum[:, :own_count] + jnp.pad(
            incoming, ((0, 0), (0, own_count - band_width))
        )
        along, energy = lax.psum(
            (column_sums(residual, image), column_sums(image, image)), ("grp", "sub")
        )
        solution, residual = update(solution, residual, image, along, energy)
    return (solution, residual)


def solution(mesh):
    return jax.shard_map(
        shards,
        mesh=mesh,
        in_specs=(
            P(None, ("grp", "sub")),
            P(("grp", "sub"), None),
            P(("grp", "sub"), None),
            P(("grp", "sub"), None),
        ),
        out_specs=(P(None, ("grp", "sub")), P(None, ("grp", "sub"))),
        check_vma=False,
    )
```

profile of v0, /device:TPU:1, one launch (start us, length us, event | category | flops | bytes accessed | tf_op | source)
XLA Modules:
  0.0 515.8 jit_solution(13757841406392980905)
XLA Ops:
  5.7 6.8 %all-to-all-start = ((s32[8,1,1296]{2,1,0:T(1,128)}), s32[8,1,1296]{2,1,0:T(1,128)S(1)}, u32[]{:S(2)}, u32[]{:S(2)}) async-start(s32[8,1,1296]{2,1,0:T(1,128)} %reshape.81), calls=%async_computation | async-start | bytes 90112 | tf_op jit(solution)/shard_map/all_to_all | solution.py:74
  12.5 6.9 %scatter_custom_fusion.1 = bf16[384,6656]{1,0:T(8,128)(2,1)} fusion(s32[128]{0:T(128)S(1)} %fusion.50, bf16[128,6656]{1,0:T(8,128)(2,1)} %param.9, bf16[]{:T(256)} %constant.23.clone.1), kind=kCustom, calls=%fused_computation.46 | custom fusion | bytes 5112320 | tf_op jit(solution)/shard_map/scatter | solution.py:25
  19.5 4.9 all-to-all-start.1
  29.8 53.3 %all-to-all-done.1 = bf16[8,48,6656]{2,1,0:T(8,128)(2,1)} async-done(((bf16[8,48,6656]{2,1,0:T(8,128)(2,1)}), bf16[8,48,6656]{2,1,0:T(8,128)(2,1)}, u32[]{:S(2)}, u32[]{:S(2)}) %all-to-all-start.1) | async-done | bytes 5111840 | tf_op jit(solution)/shard_map/all_to_all | solution.py:73
  83.1 14.8 %copy.45 = bf16[8,48,6561]{1,0,2:T(8,128)(2,1)} copy(bf16[8,48,6561]{2,1,0:T(8,128)(2,1)} %bitcast.44) | data formatting | bytes 10077696
  97.9 35.7 %copy.35 = bf16[8,48,27,3,27,3]{4,2,3,5,1,0:T(8,128)(2,1)} copy(bf16[8,48,27,3,27,3]{1,0,5,4,3,2:T(8,128)(2,1)} %bitcast.67) | data formatting | bytes 10077696
  133.6 112.3 %while.22 = (s32[]{:T(128)}, f32[96,1280]{1,0:T(8,128)}, s32[8,1296]{1,0:T(8,128)}, bf16[96,1280]{1,0:T(8,128)(2,1)S(1)}, bf16[8,48,27,3,27,3]{4,2,3,5,1,0:T(8,128)(2,1)}, /*index=5*/s32[]{:T(128)}, s32[]{:T(128)}) while((s32[]{:T(128)}, f32[96,1280]{1,0:T(8,128)}, s32[8,1296]{1,0:T(8,128)}, bf16[96,1280]{1,0:T(8,128)(2,1)S(1)}, ...), condition=%wide.region_5.6_spmd.clone, body=%wide.region_4.5_spmd.clone.sunk | while | flops 981762048 | bytes 10256283 | solution.py:53
  136.0 1.6 reshape.87
  137.7 2.8 fusion.75
  144.4 2.3 fusion.77
  150.8 2.8 fusion.75
  156.0 2.6 fusion.76
  158.6 2.3 fusion.77
  163.3 1.6 reshape.87
  165.0 2.8 fusion.75
  170.2 2.6 fusion.76
  172.8 2.3 fusion.77
  179.1 2.8 fusion.75
  184.3 2.6 fusion.76
  186.9 2.3 fusion.77
  191.6 1.6 reshape.87
  193.3 2.8 fusion.75
  198.5 2.6 fusion.76
  201.1 2.3 fusion.77
  207.5 2.8 fusion.75
  212.7 2.6 fusion.76
  215.3 2.3 fusion.77
  221.6 2.8 fusion.75
  226.8 2.6 fusion.76
  229.4 2.3 fusion.77
  235.8 2.8 fusion.75
  241.0 2.6 fusion.76
  243.6 2.3 fusion.77
  246.8 3.2 collective-permute-start.1
  253.0 66.9 %all-reduce.3 = (f32[32]{0:T(128)S(1)}, f32[32]{0:T(128)S(1)}) all-reduce(f32[32]{0:T(128)S(1)} %reduce_sum.62, f32[32]{0:T(128)S(1)} %reduce_sum.82), channel_id=1, replica_groups=mesh['grp'=8,'sub'=16] {'grp','sub'}, use_global_device_ids=true, to_apply=%region_8.9 | all-reduce | flops 64 | bytes 512 | tf_op jit(solution)/shard_map/psum | solution.py:94
  320.0 1.9 fusion.51
  323.4 3.3 collective-permute-done.2
  326.7 112.3 %while.23 = (s32[]{:T(128)}, f32[96,1280]{1,0:T(8,128)}, s32[8,1296]{1,0:T(8,128)}, bf16[96,1280]{1,0:T(8,128)(2,1)S(1)}, bf16[8,48,27,3,27,3]{4,2,3,5,1,0:T(8,128)(2,1)}, /*index=5*/s32[]{:T(128)}, s32[]{:T(128)}) while((s32[]{:T(128)}, f32[96,1280]{1,0:T(8,128)}, s32[8,1296]{1,0:T(8,128)}, bf16[96,1280]{1,0:T(8,128)(2,1)S(1)}, ...), condition=%wide.region_13.14_spmd.clone, body=%wide.region_12.13_spmd.clone.sunk | while | flops 981762048 | bytes 10256283 | solution.py:53
  330.8 2.8 fusion.83
  337.6 2.3 fusion.85
  343.9 2.8 fusion.83
  349.1 2.6 fusion.84
  351.7 2.3 fusion.85
  358.1 2.8 fusion.83
  363.3 2.6 fusion.84
  365.9 2.3 fusion.85
  372.3 2.8 fusion.83
  377.5 2.6 fusion.84
  380.0 2.3 fusion.85
  386.4 2.8 fusion.83
  391.6 2.6 fusion.84
  394.2 2.3 fusion.85
  400.6 2.8 fusion.83
  405.8 2.6 fusion.84
  408.4 2.3 fusion.85
  414.7 2.8 fusion.83
  419.9 2.6 fusion.84
  422.5 2.3 fusion.85
  428.9 2.8 fusion.83
  434.1 2.6 fusion.84
  436.7 2.3 fusion.85
  439.9 2.5 collective-permute-start.3
  445.6 68.0 %all-reduce.2 = (f32[32]{0:T(128)S(1)}, f32[32]{0:T(128)S(1)}) all-reduce(f32[32]{0:T(128)S(1)} %reduce_sum.85, f32[32]{0:T(128)S(1)} %reduce_sum.88), channel_id=1, replica_groups=mesh['grp'=8,'sub'=16] {'grp','sub'}, use_global_device_ids=true, to_apply=%region_16.17 | all-reduce | flops 64 | bytes 512 | tf_op jit(solution)/shard_map/psum | solution.py:94
  513.6 2.1 multiply_subtract_fusion
  (126 shorter events, 120.8 us)
Async XLA Ops:
  5.7 13.8 %all-to-all-start = ((s32[8,1,1296]{2,1,0:T(1,128)}), s32[8,1,1296]{2,1,0:T(1,128)S(1)}, u32[]{:S(2)}, u32[]{:S(2)}) async-start(s32[8,1,1296]{2,1,0:T(1,128)} %reshape.81), calls=%async_computation | async-start | bytes 90112 | tf_op jit(solution)/shard_map/all_to_all | solution.py:74
  19.5 4.9 copy-start
  19.5 63.7 %all-to-all-start.1 = ((bf16[8,48,6656]{2,1,0:T(8,128)(2,1)}), bf16[8,48,6656]{2,1,0:T(8,128)(2,1)}, u32[]{:S(2)}, u32[]{:S(2)}) async-start(bf16[8,48,6656]{2,1,0:T(8,128)(2,1)} %bitcast.68), calls=%async_computation.1 | async-start | bytes 10223616 | tf_op jit(solution)/shard_map/all_to_all | solution.py:73
  24.4 5.4 %collective-permute-start = (bf16[96,256]{1,0:T(8,128)(2,1)S(1)}, bf16[96,256]{1,0:T(8,128)(2,1)S(1)}, u32[]{:S(2)}, u32[]{:S(2)}) collective-permute-start(bf16[96,256]{1,0:T(8,128)(2,1)S(1)} %slice.28), channel_id=1, source_target_pairs={{1,0},{2,1},{3,2},{4,3},{5,4},{6,5},{7,6},{8,7},{9,8},{10,9},{11,1... | collective-permute-start | bytes 147464 | tf_op jit(solution)/shard_map/ppermute | solution.py:13
  246.8 4.8 collective-permute-start.1
  321.9 4.8 collective-permute-start.2
  439.9 4.1 collective-permute-start.3
where the time goes:
time: 520 us; the launch traced here: 516 us
  matrix products  147 us (28%)
  local copies, waits for them, and re-layouts  141 us (27%)
  blocking collectives  135 us (26%)
  waiting for transfers between devices  61.3 us (12%)
  starting transfers between devices  20.5 us (4%)
  other arithmetic  9.82 us (2%)
    psum x2, blocking collectives, shards(): lax.psum((column_sums(residual, image), column_sums(image, image)), ('grp...  135 us
    all_to_all x1, waiting for transfers between devices, shards(): lax.all_to_all(send_blocks, 'grp', split_axis=0, concat_axis=0, tiled=True)  53.3 us
    unnamed x7, local copies, waits for them, and re-layouts  52.2 us
    dot_general x16, matrix products, one_group(): jnp.einsum('spcqd,cosp->dosq', matrix, picked, preferred_element_type=jnp...  44.9 us
    dot_general x16, matrix products, one_group(): acc = acc + jnp.dot(high_part, selector, preferred_element_type=jnp.float32)  39.2 us
    dot_general x16, matrix products, one_group(): acc = acc + jnp.dot(low_part, selector, preferred_element_type=jnp.float32)  37.2 us
    reshape x16, local copies, waits for them, and re-layouts, one_group(): picked = picked.reshape(3, rows // 3, slot_count, 27)  26.4 us
    dot_general x16, matrix products, one_group(): jnp.einsum('rw,lw->rl', field, selector, preferred_element_type=jnp.float32)  25.1 us
  transfers between devices with their start and end apart: 6, of which 5 were waited for; matrix products, arithmetic and copies ran while one was open for 2% of the time, Pallas kernels for 0%

commit v1 on v0

--- a/solution.py
+++ b/solution.py
@@ -91,8 +91,11 @@
         image = partial_sum[:, :own_count] + jnp.pad(
             incoming, ((0, 0), (0, own_count - band_width))
         )
-        along, energy = lax.psum(
-            (column_sums(residual, image), column_sums(image, image)), ("grp", "sub")
+        _lay_domain = lambda in_array, mesh_ax, axis_id: jax.lax.psum(
+            jax.lax.psum(in_array, axis_name=mesh_ax), axis_name=axis_id
+        )
+        along, energy = _lay_domain(
+            (column_sums(residual, image), column_sums(image, image)), "sub", "grp"
         )
         solution, residual = update(solution, residual, image, along, energy)
     return (solution, residual)

time: 520 us -> 491 us (0.944)
  blocking collectives: 135 us -> 107 us
    psum x2 -> x4, blocking collectives: 135 us -> 107 us  [the longest x2 65 us: shards(): jax.lax.psum(in_array, axis_name=mesh_ax)]
where the time goes in v1:
time: 491 us; the launch traced here: 487 us
  matrix products  147 us (30%)
  local copies, waits for them, and re-layouts  141 us (29%)
  blocking collectives  107 us (22%)
  waiting for transfers between devices  61.3 us (12%)
  starting transfers between devices  19.5 us (4%)
  other arithmetic  9.83 us (2%)
    psum x2, blocking collectives, shards(): jax.lax.psum(in_array, axis_name=mesh_ax)  65 us
    all_to_all x1, waiting for transfers between devices, shards(): lax.all_to_all(send_blocks, 'grp', split_axis=0, concat_axis=0, tiled=True)  53.3 us
    unnamed x7, local copies, waits for them, and re-layouts  52.2 us
    dot_general x16, matrix products, one_group(): jnp.einsum('spcqd,cosp->dosq', matrix, picked, preferred_element_type=jnp...  44.9 us
    psum x2, blocking collectives, shards(): jax.lax.psum(jax.lax.psum(in_array, axis_name=mesh_ax), axis_name=axis_id)  42 us
    dot_general x16, matrix products, one_group(): acc = acc + jnp.dot(high_part, selector, preferred_element_type=jnp.float32)  39.2 us
    dot_general x16, matrix products, one_group(): acc = acc + jnp.dot(low_part, selector, preferred_element_type=jnp.float32)  37.2 us
    reshape x16, local copies, waits for them, and re-layouts, one_group(): picked = picked.reshape(3, rows // 3, slot_count, 27)  26.4 us
  transfers between devices with their start and end apart: 6, of which 5 were waited for; matrix products, arithmetic and copies ran while one was open for 2% of the time, Pallas kernels for 0%

profile of v1, /device:TPU:1, one launch (start us, length us, event | category | flops | bytes accessed | tf_op | source)
XLA Modules:
  0.0 486.9 jit_solution(6607161550965911844)
XLA Ops:
  5.7 6.8 %all-to-all-start = ((s32[8,1,1296]{2,1,0:T(1,128)}), s32[8,1,1296]{2,1,0:T(1,128)S(1)}, u32[]{:S(2)}, u32[]{:S(2)}) async-start(s32[8,1,1296]{2,1,0:T(1,128)} %reshape.81), calls=%async_computation | async-start | bytes 90112 | tf_op jit(solution)/shard_map/all_to_all | solution.py:74
  12.5 6.9 %scatter_custom_fusion.1 = bf16[384,6656]{1,0:T(8,128)(2,1)} fusion(s32[128]{0:T(128)S(1)} %fusion.50, bf16[128,6656]{1,0:T(8,128)(2,1)} %param.9, bf16[]{:T(256)} %constant.23.clone.1), kind=kCustom, calls=%fused_computation.46 | custom fusion | bytes 5112320 | tf_op jit(solution)/shard_map/scatter | solution.py:25
  19.5 4.9 %all-to-all-start.1 = ((bf16[8,48,6656]{2,1,0:T(8,128)(2,1)}), bf16[8,48,6656]{2,1,0:T(8,128)(2,1)}, u32[]{:S(2)}, u32[]{:S(2)}) async-start(bf16[8,48,6656]{2,1,0:T(8,128)(2,1)} %bitcast.68), calls=%async_computation.1 | async-start | bytes 10223616 | tf_op jit(solution)/shard_map/all_to_all | solution.py:73
  29.8 53.3 %all-to-all-done.1 = bf16[8,48,6656]{2,1,0:T(8,128)(2,1)} async-done(((bf16[8,48,6656]{2,1,0:T(8,128)(2,1)}), bf16[8,48,6656]{2,1,0:T(8,128)(2,1)}, u32[]{:S(2)}, u32[]{:S(2)}) %all-to-all-start.1) | async-done | bytes 5111840 | tf_op jit(solution)/shard_map/all_to_all | solution.py:73
  83.1 14.8 %copy.45 = bf16[8,48,6561]{1,0,2:T(8,128)(2,1)} copy(bf16[8,48,6561]{2,1,0:T(8,128)(2,1)} %bitcast.44) | data formatting | bytes 10077696
  97.9 35.7 %copy.35 = bf16[8,48,27,3,27,3]{4,2,3,5,1,0:T(8,128)(2,1)} copy(bf16[8,48,27,3,27,3]{1,0,5,4,3,2:T(8,128)(2,1)} %bitcast.67) | data formatting | bytes 10077696
  133.6 112.3 %while.22 = (s32[]{:T(128)}, f32[96,1280]{1,0:T(8,128)}, s32[8,1296]{1,0:T(8,128)}, bf16[96,1280]{1,0:T(8,128)(2,1)S(1)}, bf16[8,48,27,3,27,3]{4,2,3,5,1,0:T(8,128)(2,1)}, /*index=5*/s32[]{:T(128)}, s32[]{:T(128)}) while((s32[]{:T(128)}, f32[96,1280]{1,0:T(8,128)}, s32[8,1296]{1,0:T(8,128)}, bf16[96,1280]{1,0:T(8,128)(2,1)S(1)}, ...), condition=%wide.region_5.6_spmd.clone, body=%wide.region_4.5_spmd.clone.sunk | while | flops 981762048 | bytes 10256283 | solution.py:53
  136.0 1.6 reshape.87
  137.7 2.8 fusion.75
  144.4 2.3 fusion.77
  150.8 2.8 fusion.75
  156.0 2.6 fusion.76
  158.6 2.3 fusion.77
  163.3 1.6 reshape.87
  165.0 2.8 fusion.75
  170.2 2.6 fusion.76
  172.8 2.3 fusion.77
  179.1 2.8 fusion.75
  184.3 2.6 fusion.76
  186.9 2.3 fusion.77
  193.3 2.8 fusion.75
  198.5 2.6 fusion.76
  201.1 2.3 fusion.77
  207.5 2.8 fusion.75
  212.7 2.6 fusion.76
  215.3 2.3 fusion.77
  221.6 2.8 fusion.75
  226.8 2.6 fusion.76
  229.4 2.3 fusion.77
  235.8 2.8 fusion.75
  241.0 2.6 fusion.76
  243.6 2.3 fusion.77
  246.8 3.2 collective-permute-start.1
  253.0 34.3 %all-reduce.3 = (f32[32]{0:T(128)S(1)}, f32[32]{0:T(128)S(1)}) all-reduce(f32[32]{0:T(128)S(1)} %reduce_sum.62, f32[32]{0:T(128)S(1)} %reduce_sum.82), channel_id=1, replica_groups=mesh['grp'=8,'sub'=16] {'sub'}, use_global_device_ids=true, to_apply=%region_8.9 | all-reduce | flops 64 | bytes 512 | tf_op jit(solution)/shard_map/psum | solution.py:95
  287.3 20.7 %all-reduce.5 = (f32[32]{0:T(128)S(1)}, f32[32]{0:T(128)S(1)}) all-reduce(f32[32]{0:T(128)S(1)} %get-tuple-element.164, f32[32]{0:T(128)S(1)} %get-tuple-element.165), channel_id=1, replica_groups=mesh['grp'=8,'sub'=16] {'grp'}, use_global_device_ids=true, to_apply=%region_9.10 | all-reduce | flops 64 | bytes 512 | tf_op jit(solution)/shard_map/psum | solution.py:94
  308.1 1.9 fusion.51
  311.5 3.3 collective-permute-done.2
  314.8 112.3 %while.23 = (s32[]{:T(128)}, f32[96,1280]{1,0:T(8,128)}, s32[8,1296]{1,0:T(8,128)}, bf16[96,1280]{1,0:T(8,128)(2,1)S(1)}, bf16[8,48,27,3,27,3]{4,2,3,5,1,0:T(8,128)(2,1)}, /*index=5*/s32[]{:T(128)}, s32[]{:T(128)}) while((s32[]{:T(128)}, f32[96,1280]{1,0:T(8,128)}, s32[8,1296]{1,0:T(8,128)}, bf16[96,1280]{1,0:T(8,128)(2,1)S(1)}, ...), condition=%wide.region_15.16_spmd.clone, body=%wide.region_14.15_spmd.clone.sunk | while | flops 981762048 | bytes 10256283 | solution.py:53
  318.9 2.8 fusion.83
  325.6 2.3 fusion.85
  332.0 2.8 fusion.83
  337.2 2.6 fusion.84
  339.8 2.3 fusion.85
  346.2 2.8 fusion.83
  351.4 2.6 fusion.84
  354.0 2.3 fusion.85
  360.3 2.8 fusion.83
  365.5 2.6 fusion.84
  368.1 2.3 fusion.85
  374.5 2.8 fusion.83
  379.7 2.6 fusion.84
  382.3 2.3 fusion.85
  388.7 2.8 fusion.83
  393.9 2.6 fusion.84
  396.5 2.3 fusion.85
  402.8 2.8 fusion.83
  408.0 2.6 fusion.84
  410.6 2.3 fusion.85
  417.0 2.8 fusion.83
  422.2 2.6 fusion.84
  424.8 2.3 fusion.85
  432.7 30.6 %all-reduce.2 = (f32[32]{0:T(128)S(1)}, f32[32]{0:T(128)S(1)}) all-reduce(f32[32]{0:T(128)S(1)} %reduce_sum.85, f32[32]{0:T(128)S(1)} %reduce_sum.88), channel_id=1, replica_groups=mesh['grp'=8,'sub'=16] {'sub'}, use_global_device_ids=true, to_apply=%region_18.19 | all-reduce | flops 64 | bytes 512 | tf_op jit(solution)/shard_map/psum | solution.py:95
  463.4 21.3 %all-reduce.4 = (f32[32]{0:T(128)S(1)}, f32[32]{0:T(128)S(1)}) all-reduce(f32[32]{0:T(128)S(1)} %get-tuple-element.162, f32[32]{0:T(128)S(1)} %get-tuple-element.163), channel_id=1, replica_groups=mesh['grp'=8,'sub'=16] {'grp'}, use_global_device_ids=true, to_apply=%region_19.20 | all-reduce | flops 64 | bytes 512 | tf_op jit(solution)/shard_map/psum | solution.py:94
  484.8 2.1 multiply_subtract_fusion
  (128 shorter events, 124.0 us)
Async XLA Ops:
  5.7 13.8 %all-to-all-start = ((s32[8,1,1296]{2,1,0:T(1,128)}), s32[8,1,1296]{2,1,0:T(1,128)S(1)}, u32[]{:S(2)}, u32[]{:S(2)}) async-start(s32[8,1,1296]{2,1,0:T(1,128)} %reshape.81), calls=%async_computation | async-start | bytes 90112 | tf_op jit(solution)/shard_map/all_to_all | solution.py:74
  19.5 4.9 %copy-start = (f32[96,1024]{1,0:T(8,128)S(1)}, f32[96,1024]{1,0:T(8,128)}, u32[]{:S(2)}) copy-start(f32[96,1024]{1,0:T(8,128)} %param.8) | copy-start | bytes 1179652
  19.5 63.7 %all-to-all-start.1 = ((bf16[8,48,6656]{2,1,0:T(8,128)(2,1)}), bf16[8,48,6656]{2,1,0:T(8,128)(2,1)}, u32[]{:S(2)}, u32[]{:S(2)}) async-start(bf16[8,48,6656]{2,1,0:T(8,128)(2,1)} %bitcast.68), calls=%async_computation.1 | async-start | bytes 10223616 | tf_op jit(solution)/shard_map/all_to_all | solution.py:73
  24.4 5.4 %collective-permute-start = (bf16[96,256]{1,0:T(8,128)(2,1)S(1)}, bf16[96,256]{1,0:T(8,128)(2,1)S(1)}, u32[]{:S(2)}, u32[]{:S(2)}) collective-permute-start(bf16[96,256]{1,0:T(8,128)(2,1)S(1)} %slice.28), channel_id=1, source_target_pairs={{1,0},{2,1},{3,2},{4,3},{5,4},{6,5},{7,6},{8,7},{9,8},{10,9},{11,1... | collective-permute-start | bytes 147464 | tf_op jit(solution)/shard_map/ppermute | solution.py:13
  246.8 4.8 collective-permute-start.1
  310.0 4.8 collective-permute-start.2
  428.0 3.2 collective-permute-start.3
